TPU v7x, 128 devices: a whole 4x4x4 slice. The times are simulated.
128 devices in a mesh: row: 16 (over z, y_hi, core), col: 8 (over y_lo, x).
Axes of the slice: x: 4, y: 4 (y_hi: 2, y_lo: 2; y = y_hi * 2 + y_lo), z: 4, core: 2. Of those that a mesh axis runs over, the one named last changes fastest.
Arguments:
- packed_tiles: bfloat16 [768, 128, 1024], P('row', None, 'col'), may hold values from -6 to 6
- source_pick: int32 [16, 48], P('row'), may hold values from 0 to 47, each once within a row
- owner_place: int32 [16, 48], P('row'), may hold values from 0 to 47, each once within a row
- tile_orient: int32 [16, 48], P('row'), may hold values from 0 to 3
- w_panel: bfloat16 [4096, 12288], P('row', 'col'), may hold values from -0.09375 to 0.09375
Outputs:
- particle_hole: bfloat16 [24576, 12288], P('row', 'col')
Inputs may be any that keep to these rules, and one draw needn't show every extreme that they name: `source_pick`: each row is a permutation of the stored tiles' local indices. `owner_place`: each row is a permutation of the received items.
All inputs are finite; a program needn't handle non-finite values.
Results may differ from a plain program's by a relative error of at most 0.001.
Values may be sent and summed in bfloat16 or wider, within the bound.
No kernel may reach another device: no remote copies, remote signals or barrier semaphores. Data moves between devices by JAX's collectives and lax.ppermute only.
A program may use at most 128 MiB of HBM per device.

v0:
```python
import jax
import jax.numpy as jnp
from jax import lax
from jax.sharding import PartitionSpec as P

VW = 768
KC = 512


def orient_tiles(tile_set, orient_codes):
    flipped = (jnp.remainder(orient_codes, 2) == 1)[:, None, None, None]
    negated = (orient_codes >= 2)[:, None, None, None]
    turned = jnp.where(flipped, jnp.swapaxes(tile_set, 1, 3), tile_set)
    return jnp.where(negated, -turned, turned)


def assemble(tile_set, blocks):
    tile_width = tile_set.shape[1]
    col_tiles = KC // tile_width
    row_tiles = tile_set.shape[0] // col_tiles
    tile_grid = tile_set.reshape(row_tiles, col_tiles, tile_width, blocks, tile_width)
    return tile_grid.transpose(0, 2, 3, 1, 4).reshape(
        row_tiles * tile_width, blocks * col_tiles * tile_width
    )


def antisymmetrize(product):
    height = product.shape[0]
    breadth = product.shape[1]
    blocked = product.reshape(height // VW, VW, breadth // VW, VW)
    return (blocked - blocked.transpose(0, 3, 2, 1)).reshape(height, breadth).astype(jnp.bfloat16)


def on_device(packed_tiles, source_pick, owner_place, tile_orient, w_panel):
    stored = packed_tiles.shape[0]
    tile_width = packed_tiles.shape[1]
    row_peers = lax.axis_size("row")
    peer_slots = stored // row_peers
    blocks = lax.axis_size("col")
    whole_tiles = lax.all_gather(packed_tiles, "col", axis=2, tiled=True)
    outgoing = jnp.take(whole_tiles, source_pick[0], axis=0)
    outgoing = outgoing.reshape(row_peers, peer_slots, tile_width, blocks * tile_width)
    incoming = lax.all_to_all(outgoing, "row", split_axis=0, concat_axis=0, tiled=True)
    incoming = incoming.reshape(stored, tile_width, blocks * tile_width)
    owner_tiles = jnp.take(incoming, owner_place[0], axis=0).reshape(
        stored, tile_width, blocks, tile_width
    )
    lambda_rows = assemble(orient_tiles(owner_tiles, tile_orient[0]), blocks)
    product = jnp.dot(
        lambda_rows,
        lax.all_gather(w_panel, "row", axis=0, tiled=True),
        preferred_element_type=jnp.float32,
    )
    return antisymmetrize(product)


def solution(mesh):
    in_specs = (
        P("row", None, "col"),
        P("row", None),
        P("row", None),
        P("row", None),
        P("row", "col"),
    )
    out_specs = P("row", "col")
    return jax.shard_map(
        on_device, mesh=mesh, in_specs=in_specs, out_specs=out_specs, check_vma=False
    )
```

profile of v0, /device:TPU:33, one launch (start us, length us, event | category | flops | bytes accessed | tf_op | source)
XLA Modules:
  0.0 523.9 jit_solution(2093930135659324942)
XLA Ops:
  6.5 0.7 all-gather.3.cloned.1.call-update
  7.3 0.7 all-gather.5.cloned.1.call-update
  8.0 0.7 compare_select_fusion.1
  8.7 0.7 compare_and_fusion.1
  9.3 134.3 %all-gather.3.cloned.1.call-done = bf16[48,128,1024]{2,1,0:T(8,128)(2,1)} async-done(((bf16[48,128,128]{2,1,0:T(8,128)(2,1)}), bf16[48,128,1024]{2,1,0:T(8,128)(2,1)}) %all-gather.3.cloned.1.call-update) | async-done | bytes 12582928 | tf_op jit(solution)/shard_map/all_gather | solution.py:40
  143.6 10.8 %gather_fusion = bf16[48,128,1024]{2,1,0:T(8,128)(2,1)} fusion(bf16[48,128,1024]{2,1,0:T(8,128)(2,1)} %all-gather.3.cloned.1.call-done, s32[1024]{0:T(1024)S(1)} %pad_clamp_fusion.1), kind=kCustom, calls=%fused_computation.clone | custom fusion | bytes 25166016 | tf_op jit(solution)/shard_map/jit(_take)/gather | solution.py:41
  154.5 10.8 %broadcast_select_fusion.1 = bf16[48,128,1024]{2,1,0:T(8,128)(2,1)} fusion(bf16[48,128,1024]{2,1,0:T(8,128)(2,1)} %gather_fusion, pred[48]{0:T(512)(128)(4,1)S(1)} %compare_and_fusion.1), kind=kLoop, calls=%fused_computation.8 | loop fusion | flops 6291456 | bytes 25165872 | tf_op jit(solution)/shard_map/jit(_take)/select_n | solution.py:41
  165.3 10.7 %all-to-all-start = ((bf16[16,3,128,1024]{3,2,1,0:T(8,128)(2,1)}), bf16[16,3,128,1024]{3,2,1,0:T(8,128)(2,1)}, u32[]{:S(2)}, u32[]{:S(2)}) async-start(bf16[16,3,128,1024]{3,2,1,0:T(8,128)(2,1)} %bitcast.45), calls=%async_computation | async-start | bytes 25165824 | tf_op jit(solution)/shard_map/all_to_all | solution.py:43
  176.1 166.8 %all-gather.5.cloned.1.call-done = bf16[4096,1536]{1,0:T(8,128)(2,1)} async-done(((bf16[256,1536]{1,0:T(8,128)(2,1)}), bf16[4096,1536]{1,0:T(8,128)(2,1)}) %all-gather.5.cloned.1.call-update) | async-done | bytes 12582928 | tf_op jit(solution)/shard_map/all_gather | solution.py:51
  342.8 16.7 %copy.15 = bf16[1536,4096]{1,0:T(8,128)(2,1)} copy(bf16[1536,4096]{0,1:T(8,128)(2,1)} %bitcast.49) | data formatting | bytes 25165824 | tf_op jit(solution)/shard_map/dot_general | solution.py:49
  359.6 10.8 %gather_fusion.1 = bf16[48,128,1024]{2,1,0:T(8,128)(2,1)} fusion(bf16[48,128,1024]{2,1,0:T(8,128)(2,1)} %bitcast.4, s32[1024]{0:T(1024)S(1)} %pad_clamp_fusion), kind=kCustom, calls=%fused_computation.1.clone | custom fusion | bytes 25166016 | tf_op jit(solution)/shard_map/jit(_take)/gather | solution.py:45
  370.4 6.5 %broadcast_select_fusion = bf16[48,128,1024]{2,1,0:T(8,128)(2,1)S(1)} fusion(bf16[48,128,1024]{2,1,0:T(8,128)(2,1)} %gather_fusion.1, pred[48]{0:T(512)(128)(4,1)S(1)} %compare_and_fusion), kind=kLoop, calls=%fused_computation.7 | loop fusion | flops 6291456 | bytes 25165872 | tf_op jit(solution)/shard_map/jit(_take)/select_n | solution.py:45
  376.9 2.9 copy.19
  379.8 4.5 copy-done
  384.3 5.0 bitcast_bitcast_fusion
  389.3 17.9 %copy.13 = bf16[48,128,8,128]{3,2,1,0:T(8,128)(2,1)} copy(bf16[48,128,8,128]{1,2,3,0:T(8,128)(2,1)} %bitcast_bitcast_fusion) | data formatting | bytes 25165824 | tf_op jit(solution)/shard_map/transpose | solution.py:13
  407.2 9.3 %negate_select_fusion = bf16[48,128,8,128]{3,2,1,0:T(8,128)(2,1)S(1)} fusion(bf16[48,128,8,128]{3,2,1,0:T(8,128)(2,1)} %copy.13, pred[48]{0:T(512)(128)(4,1)S(1)} %get-tuple-element.7, pred[48]{0:T(512)(128)(4,1)S(1)} %get-tuple-element.6, bf16[48,128,8,128]{3,2,1,0:T(8,128)(2,1)} %bitcast.44), kind=kLoop, calls=%fused_computation.2 | loop fusion | flops 18874368 | bytes 37748832 | tf_op jit(solution)/shard_map/jit(_where)/select_n | solution.py:14
  416.5 17.1 %copy.14 = bf16[12,128,8,4,128]{4,3,2,1,0:T(4,128)(2,1)} copy(bf16[12,128,8,4,128]{4,2,1,3,0:T(8,128)(2,1)S(1)} %bitcast.46) | data formatting | bytes 25165824 | tf_op jit(solution)/shard_map/transpose | solution.py:22
  433.6 21.1 %reshape.77 = bf16[2,768,4096,1]{2,1,0,3:T(8,128)(2,1)} reshape(bf16[12,128,8,4,128]{4,3,2,1,0:T(4,128)(2,1)} %copy.14) | data formatting | bytes 25165824 | tf_op jit(solution)/shard_map/dot_general | solution.py:49
  454.7 27.9 %fusion = f32[2,768,2,768]{3,1,2,0:T(8,128)} fusion(bf16[2,768,4096,1]{2,1,0,3:T(8,128)(2,1)} %bitcast.50, bf16[2,768,4096,1]{2,1,0,3:T(8,128)(2,1)} %reshape.77), kind=kOutput, calls=%fused_computation.5 | convolution fusion | flops 19327352832 | bytes 34603008 | tf_op jit(solution)/shard_map/dot_general | solution.py:49
  482.6 9.7 %copy.16 = f32[2,768,2,768]{1,3,2,0:T(8,128)} copy(f32[2,768,2,768]{3,1,2,0:T(8,128)} %fusion) | data formatting | bytes 18874368 | tf_op jit(solution)/shard_map/dot_general | solution.py:49
  492.2 10.0 %fusion.2 = bf16[2,768,2,768]{3,1,2,0:T(8,128)(2,1)} fusion(f32[2,768,2,768]{3,1,2,0:T(8,128)} %fusion, f32[2,768,2,768]{1,3,2,0:T(8,128)} %copy.16), kind=kLoop, calls=%fused_computation.10 | loop fusion | flops 4718592 | bytes 23592960 | tf_op jit(solution)/shard_map/convert_element_type | solution.py:31
  502.3 9.3 %copy.17 = bf16[2,768,2,768]{3,2,1,0:T(2,128)(2,1)} copy(bf16[2,768,2,768]{3,1,2,0:T(8,128)(2,1)} %fusion.2) | data formatting | bytes 9437184 | tf_op jit(solution)/shard_map/convert_element_type | solution.py:31
  511.6 5.5 %copy.20 = bf16[192,8,2,768]{3,1,2,0:T(8,128)(2,1)} copy(bf16[192,8,2,768]{3,2,1,0:T(2,128)(2,1)} %bitcast.48) | data formatting | bytes 9437184
  (13 shorter events, 0.1 us)
Async XLA Ops:
  6.5 137.1 %all-gather.3.cloned.1.call-start = ((), (), s32[]{:S(2)}) async-start(), calls=%async_computation.1 | async-start | bytes 14155776 | tf_op jit(solution)/shard_map/all_gather | solution.py:40
  7.3 335.6 %all-gather.5.cloned.1.call-start = ((), (), s32[]{:S(2)}) async-start(), calls=%async_computation.2 | async-start | bytes 13369344 | tf_op jit(solution)/shard_map/all_gather | solution.py:51
  165.3 10.7 %copy-start.1 = (s32[1,48]{1,0:T(1,128)S(1)}, s32[1,48]{1,0:T(1,128)}, u32[]{:S(2)}) copy-start(s32[1,48]{1,0:T(1,128)} %param.9) | copy-start | bytes 580
  165.3 10.8 %copy-start.2 = (s32[1,48]{1,0:T(1,128)S(1)}, s32[1,48]{1,0:T(1,128)}, u32[]{:S(2)}) copy-start(s32[1,48]{1,0:T(1,128)} %param.10) | copy-start | bytes 580
  165.3 194.3 %all-to-all-start = ((bf16[16,3,128,1024]{3,2,1,0:T(8,128)(2,1)}), bf16[16,3,128,1024]{3,2,1,0:T(8,128)(2,1)}, u32[]{:S(2)}, u32[]{:S(2)}) async-start(bf16[16,3,128,1024]{3,2,1,0:T(8,128)(2,1)} %bitcast.45), calls=%async_computation | async-start | bytes 25165824 | tf_op jit(solution)/shard_map/all_to_all | solution.py:43
  379.8 4.5 copy-start
Sparse Core Ops, SparseCore 0:
  8.9 134.6 all-gather.2
  146.1 196.7 all-gather.4
where the time goes:
time: 526 us; the launch traced here: 524 us
  waiting for transfers between devices  302 us (57%)
  local copies, waits for them, and re-layouts  131 us (25%)
  other arithmetic  38.1 us (7%)
  matrix products  27.9 us (5%)
  between operations  13.5 us (3%)
  starting transfers between devices  10.8 us (2%)
    all_gather x1, waiting for transfers between devices, on_device(): lax.all_gather(w_panel, 'row', axis=0, tiled=True)  167 us
    all_gather x1, waiting for transfers between devices, on_device(): whole_tiles = lax.all_gather(packed_tiles, 'col', axis=2, tiled=True)  134 us
    dot_general x3, local copies, waits for them, and re-layouts, on_device(): jnp.dot(lambda_rows, lax.all_gather(w_panel, 'row', axis=0, tiled=True),...  47.5 us
    dot_general x1, matrix products, on_device(): jnp.dot(lambda_rows, lax.all_gather(w_panel, 'row', axis=0, tiled=True),...  27.9 us
    transpose x2, local copies, waits for them, and re-layouts, orient_tiles(): turned = jnp.where(flipped, jnp.swapaxes(tile_set, 1, 3), tile_set)  22.9 us
    transpose x1, local copies, waits for them, and re-layouts, assemble(): tile_grid.transpose(0, 2, 3, 1, 4)  17.1 us
    unnamed x8, local copies, waits for them, and re-layouts  12.8 us
    select_n x2, other arithmetic, on_device(): outgoing = jnp.take(whole_tiles, source_pick[0], axis=0)  11.5 us
  transfers between devices with their start and end apart: 3, of which 2 were waited for; matrix products, arithmetic and copies ran while one was open for 8% of the time, Pallas kernels for 0%

commit v1 on v0

--- a/solution.py
+++ b/solution.py
@@ -5,6 +5,13 @@
 
 VW = 768
 KC = 512
+
+
+def _mark_types(body):
+    right_arr = jnp.concatenate(
+        lax.all_to_all(jnp.stack([body for _ in range(lax.axis_size("row"))], 0), "row", 0, 0), 0
+    )
+    return right_arr
 
 
 def orient_tiles(tile_set, orient_codes):
@@ -46,11 +53,7 @@
         stored, tile_width, blocks, tile_width
     )
     lambda_rows = assemble(orient_tiles(owner_tiles, tile_orient[0]), blocks)
-    product = jnp.dot(
-        lambda_rows,
-        lax.all_gather(w_panel, "row", axis=0, tiled=True),
-        preferred_element_type=jnp.float32,
-    )
+    product = jnp.dot(lambda_rows, _mark_types(w_panel), preferred_element_type=jnp.float32)
     return antisymmetrize(product)
 
 

time: 526 us -> 595 us (1.13)
  waiting for transfers between devices: 302 us -> 342 us
  local copies, waits for them, and re-layouts: 131 us -> 154 us
    all_gather x1 -> x0, waiting for transfers between devices: 167 us -> none  [on_device(): lax.all_gather(w_panel, 'row', axis=0, tiled=True)]
    all_to_all x0 -> x1, waiting for transfers between devices: none -> 114 us  [_mark_types(): lax.all_to_all(jnp.stack([body for _ in range(lax.axis_size('row'))], 0),...]
    all_to_all x1, waiting for transfers between devices: 0.01 us -> 107 us  [on_device(): lax.all_to_all(outgoing, 'row', split_axis=0, concat_axis=0, tiled=True)]
    all_to_all x0 -> x1, local copies, waits for them, and re-layouts: none -> 16 us  [_mark_types(): lax.all_to_all(jnp.stack([body for _ in range(lax.axis_size('row'))], 0),...]
    all_gather x1, waiting for transfers between devices: 134 us -> 121 us  [on_device(): whole_tiles = lax.all_gather(packed_tiles, 'col', axis=2, tiled=True)]
    all_to_all x0 -> x1, starting transfers between devices: none -> 8.48 us  [_mark_types(): lax.all_to_all(jnp.stack([body for _ in range(lax.axis_size('row'))], 0),...]
    unnamed x8 -> x11, local copies, waits for them, and re-layouts: 12.8 us -> 14.2 us
  transfers between devices with their start and end apart: 3 -> 3, of which waited for: 2 -> 3; matrix products, arithmetic and copies ran while one was open for 8% -> 10% of each run, Pallas kernels for 0% -> 0%
where the time goes in v1:
time: 595 us; the launch traced here: 590 us
  waiting for transfers between devices  342 us (57%)
  local copies, waits for them, and re-layouts  154 us (26%)
  other arithmetic  36.6 us (6%)
  matrix products  27.9 us (5%)
  starting transfers between devices  15.5 us (3%)
  between operations  13.5 us (2%)
    all_gather x1, waiting for transfers between devices, on_device(): whole_tiles = lax.all_gather(packed_tiles, 'col', axis=2, tiled=True)  121 us
    all_to_all x1, waiting for transfers between devices, _mark_types(): lax.all_to_all(jnp.stack([body for _ in range(lax.axis_size('row'))], 0),...  114 us
    all_to_all x1, waiting for transfers between devices, on_device(): lax.all_to_all(outgoing, 'row', split_axis=0, concat_axis=0, tiled=True)  107 us
    dot_general x3, local copies, waits for them, and re-layouts, on_device(): jnp.dot(lambda_rows, _mark_types(w_panel), preferred_element_type=jnp.flo...  47.5 us
    dot_general x1, matrix products, on_device(): jnp.dot(lambda_rows, _mark_types(w_panel), preferred_element_type=jnp.flo...  27.9 us
    transpose x2, local copies, waits for them, and re-layouts, orient_tiles(): turned = jnp.where(flipped, jnp.swapaxes(tile_set, 1, 3), tile_set)  22.9 us
    transpose x1, local copies, waits for them, and re-layouts, assemble(): tile_grid.transpose(0, 2, 3, 1, 4)  17.1 us
    all_to_all x1, local copies, waits for them, and re-layouts, _mark_types(): lax.all_to_all(jnp.stack([body for _ in range(lax.axis_size('row'))], 0),...  16 us
  transfers between devices with their start and end apart: 3, of which 3 were waited for; matrix products, arithmetic and copies ran while one was open for 10% of the time, Pallas kernels for 0%

profile of v1, /device:TPU:33, one launch (start us, length us, event | category | flops | bytes accessed | tf_op | source)
XLA Modules:
  0.0 590.0 jit_solution(7021249298388788624)
XLA Ops:
  8.7 5.7 stack.2
  14.3 8.5 %all-to-all-start.1 = ((bf16[16,256,1536]{1,2,0:T(8,128)(2,1)}), bf16[16,256,1536]{1,2,0:T(8,128)(2,1)}, u32[]{:S(2)}, u32[]{:S(2)}) async-start(bf16[16,256,1536]{1,2,0:T(8,128)(2,1)} %stack.2), calls=%async_computation.1 | async-start | bytes 25165824 | tf_op jit(solution)/shard_map/all_to_all | solution.py:12
  22.9 120.6 %all-gather.2.cloned.1.call-done = bf16[48,128,1024]{2,1,0:T(8,128)(2,1)} async-done(((bf16[48,128,128]{2,1,0:T(8,128)(2,1)}), bf16[48,128,1024]{2,1,0:T(8,128)(2,1)}) %all-gather.2.cloned.1.call-update) | async-done | bytes 12582928 | tf_op jit(solution)/shard_map/all_gather | solution.py:47
  143.5 10.8 %gather_fusion = bf16[48,128,1024]{2,1,0:T(8,128)(2,1)} fusion(bf16[48,128,1024]{2,1,0:T(8,128)(2,1)} %all-gather.2.cloned.1.call-done, s32[1024]{0:T(1024)S(1)} %pad_clamp_fusion.1), kind=kCustom, calls=%fused_computation.clone | custom fusion | bytes 25166016 | tf_op jit(solution)/shard_map/jit(_take)/gather | solution.py:48
  154.3 10.7 %broadcast_select_fusion.1 = bf16[48,128,1024]{2,1,0:T(8,128)(2,1)} fusion(bf16[48,128,1024]{2,1,0:T(8,128)(2,1)} %gather_fusion, pred[48]{0:T(512)(128)(4,1)S(1)} %compare_and_fusion.1), kind=kLoop, calls=%fused_computation.8 | loop fusion | flops 6291456 | bytes 25165872 | tf_op jit(solution)/shard_map/jit(_take)/select_n | solution.py:48
  165.0 113.9 %all-to-all-done.1 = bf16[16,256,1536]{1,2,0:T(8,128)(2,1)} async-done(((bf16[16,256,1536]{1,2,0:T(8,128)(2,1)}), bf16[16,256,1536]{1,2,0:T(8,128)(2,1)}, u32[]{:S(2)}, u32[]{:S(2)}) %all-to-all-start.1) | async-done | bytes 12582944 | tf_op jit(solution)/shard_map/all_to_all | solution.py:12
  279.0 7.0 %all-to-all-start = ((bf16[16,3,128,1024]{3,2,1,0:T(8,128)(2,1)}), bf16[16,3,128,1024]{3,2,1,0:T(8,128)(2,1)}, u32[]{:S(2)}, u32[]{:S(2)}) async-start(bf16[16,3,128,1024]{3,2,1,0:T(8,128)(2,1)} %bitcast.48), calls=%async_computation | async-start | bytes 25165824 | tf_op jit(solution)/shard_map/all_to_all | solution.py:50
  286.0 16.0 %copy.26 = bf16[16,256,1536]{2,1,0:T(8,128)(2,1)} copy(bf16[16,256,1536]{1,2,0:T(8,128)(2,1)} %all-to-all-done.1) | data formatting | bytes 25165824 | tf_op jit(solution)/shard_map/all_to_all | solution.py:12
  302.0 16.7 %copy.27 = bf16[1536,4096]{1,0:T(8,128)(2,1)} copy(bf16[1536,4096]{0,1:T(8,128)(2,1)} %bitcast.47) | data formatting | bytes 25165824 | tf_op jit(solution)/shard_map/dot_general | solution.py:56
  318.8 106.8 %all-to-all-done = bf16[16,3,128,1024]{3,2,1,0:T(8,128)(2,1)} async-done(((bf16[16,3,128,1024]{3,2,1,0:T(8,128)(2,1)}), bf16[16,3,128,1024]{3,2,1,0:T(8,128)(2,1)}, u32[]{:S(2)}, u32[]{:S(2)}) %all-to-all-start) | async-done | bytes 12582944 | tf_op jit(solution)/shard_map/all_to_all | solution.py:50
  425.5 11.0 %gather_fusion.1 = bf16[48,128,1024]{2,1,0:T(8,128)(2,1)} fusion(bf16[48,128,1024]{2,1,0:T(8,128)(2,1)} %bitcast.4, s32[1024]{0:T(1024)S(1)} %pad_clamp_fusion), kind=kCustom, calls=%fused_computation.1.clone | custom fusion | bytes 25166016 | tf_op jit(solution)/shard_map/jit(_take)/gather | solution.py:52
  436.5 6.5 %broadcast_select_fusion = bf16[48,128,1024]{2,1,0:T(8,128)(2,1)S(1)} fusion(bf16[48,128,1024]{2,1,0:T(8,128)(2,1)} %gather_fusion.1, pred[48]{0:T(512)(128)(4,1)S(1)} %compare_and_fusion), kind=kLoop, calls=%fused_computation.7 | loop fusion | flops 6291456 | bytes 25165872 | tf_op jit(solution)/shard_map/jit(_take)/select_n | solution.py:52
  443.0 2.9 copy.31
  445.9 4.5 copy-done
  450.4 5.0 bitcast_bitcast_fusion
  455.4 17.9 %copy.23 = bf16[48,128,8,128]{3,2,1,0:T(8,128)(2,1)} copy(bf16[48,128,8,128]{1,2,3,0:T(8,128)(2,1)} %bitcast_bitcast_fusion) | data formatting | bytes 25165824 | tf_op jit(solution)/shard_map/transpose | solution.py:20
  473.2 9.3 %negate_select_fusion = bf16[48,128,8,128]{3,2,1,0:T(8,128)(2,1)S(1)} fusion(bf16[48,128,8,128]{3,2,1,0:T(8,128)(2,1)} %copy.23, pred[48]{0:T(512)(128)(4,1)S(1)} %get-tuple-element.7, pred[48]{0:T(512)(128)(4,1)S(1)} %get-tuple-element.6, bf16[48,128,8,128]{3,2,1,0:T(8,128)(2,1)} %bitcast.46), kind=kLoop, calls=%fused_computation.2 | loop fusion | flops 18874368 | bytes 37748832 | tf_op jit(solution)/shard_map/jit(_where)/select_n | solution.py:21
  482.6 17.1 %copy.24 = bf16[12,128,8,4,128]{4,3,2,1,0:T(4,128)(2,1)} copy(bf16[12,128,8,4,128]{4,2,1,3,0:T(8,128)(2,1)S(1)} %bitcast.49) | data formatting | bytes 25165824 | tf_op jit(solution)/shard_map/transpose | solution.py:29
  499.6 21.1 %reshape.83 = bf16[2,768,4096,1]{2,1,0,3:T(8,128)(2,1)} reshape(bf16[12,128,8,4,128]{4,3,2,1,0:T(4,128)(2,1)} %copy.24) | data formatting | bytes 25165824 | tf_op jit(solution)/shard_map/dot_general | solution.py:56
  520.8 27.9 %fusion = f32[2,768,2,768]{3,1,2,0:T(8,128)} fusion(bf16[2,768,4096,1]{2,1,0,3:T(8,128)(2,1)} %bitcast.52, bf16[2,768,4096,1]{2,1,0,3:T(8,128)(2,1)} %reshape.83), kind=kOutput, calls=%fused_computation.5 | convolution fusion | flops 19327352832 | bytes 34603008 | tf_op jit(solution)/shard_map/dot_general | solution.py:56
  548.6 9.7 %copy.28 = f32[2,768,2,768]{1,3,2,0:T(8,128)} copy(f32[2,768,2,768]{3,1,2,0:T(8,128)} %fusion) | data formatting | bytes 18874368 | tf_op jit(solution)/shard_map/dot_general | solution.py:56
  558.3 10.0 %fusion.2 = bf16[2,768,2,768]{3,1,2,0:T(8,128)(2,1)} fusion(f32[2,768,2,768]{3,1,2,0:T(8,128)} %fusion, f32[2,768,2,768]{1,3,2,0:T(8,128)} %copy.28), kind=kLoop, calls=%fused_computation.10 | loop fusion | flops 4718592 | bytes 23592960 | tf_op jit(solution)/shard_map/convert_element_type | solution.py:38
  568.3 9.3 %copy.29 = bf16[2,768,2,768]{3,2,1,0:T(2,128)(2,1)} copy(bf16[2,768,2,768]{3,1,2,0:T(8,128)(2,1)} %fusion.2) | data formatting | bytes 9437184 | tf_op jit(solution)/shard_map/convert_element_type | solution.py:38
  577.7 5.5 copy.32
  (17 shorter events, 2.2 us)
Async XLA Ops:
  6.5 136.9 %all-gather.2.cloned.1.call-start = ((), (), s32[]{:S(2)}) async-start(), calls=%async_computation.2 | async-start | bytes 14155776 | tf_op jit(solution)/shard_map/all_gather | solution.py:47
  14.3 8.5 %copy-start.1 = (s32[1,48]{1,0:T(1,128)S(1)}, s32[1,48]{1,0:T(1,128)}, u32[]{:S(2)}) copy-start(s32[1,48]{1,0:T(1,128)} %param.8) | copy-start | bytes 580
  14.3 264.6 %all-to-all-start.1 = ((bf16[16,256,1536]{1,2,0:T(8,128)(2,1)}), bf16[16,256,1536]{1,2,0:T(8,128)(2,1)}, u32[]{:S(2)}, u32[]{:S(2)}) async-start(bf16[16,256,1536]{1,2,0:T(8,128)(2,1)} %stack.2), calls=%async_computation.1 | async-start | bytes 25165824 | tf_op jit(solution)/shard_map/all_to_all | solution.py:12
  279.0 7.0 %copy-start.2 = (s32[1,48]{1,0:T(1,128)S(1)}, s32[1,48]{1,0:T(1,128)}, u32[]{:S(2)}) copy-start(s32[1,48]{1,0:T(1,128)} %param.9) | copy-start | bytes 580
  279.0 7.1 %copy-start.3 = (s32[1,48]{1,0:T(1,128)S(1)}, s32[1,48]{1,0:T(1,128)}, u32[]{:S(2)}) copy-start(s32[1,48]{1,0:T(1,128)} %param.10) | copy-start | bytes 580
  279.0 146.5 %all-to-all-start = ((bf16[16,3,128,1024]{3,2,1,0:T(8,128)(2,1)}), bf16[16,3,128,1024]{3,2,1,0:T(8,128)(2,1)}, u32[]{:S(2)}, u32[]{:S(2)}) async-start(bf16[16,3,128,1024]{3,2,1,0:T(8,128)(2,1)} %bitcast.48), calls=%async_computation | async-start | bytes 25165824 | tf_op jit(solution)/shard_map/all_to_all | solution.py:50
  445.9 4.5 copy-start
Sparse Core Ops, SparseCore 0:
  8.9 134.5 all-gather.1
